TPU v7x, 128 devices: a whole 4x4x4 slice. The times are simulated.
128 devices in a mesh: tok: 8 (over z_hi, x), wid: 16 (over z_lo, y, core).
Axes of the slice: x: 4, y: 4, z: 4 (z_hi: 2, z_lo: 2; z = z_hi * 2 + z_lo), core: 2. Of those that a mesh axis runs over, the one named last changes fastest.
Arguments:
- resident_x: float32 [16384, 16384], P('tok', 'wid'), may hold values from -0.53033006 to 0.53033006
- resident_g: float32 [16384, 16384], P('tok', 'wid'), may hold values from -0.53033006 to 0.53033006
- query_x: float32 [1024, 16384], P('tok', 'wid'), may hold values from -0.53033006 to 0.53033006
- query_g: float32 [1024, 16384], P('tok', 'wid'), may hold values from -0.53033006 to 0.53033006
Outputs:
- kernel: float32 [16384, 1024], P(('tok', 'wid'))
All inputs are finite; a program needn't handle non-finite values.
Results may differ from a plain program's by a relative error of at most 0.0002.
Values sent between devices are 32-bit elements; how exact they have to be, the bound alone decides.
A program may use at most 128 MiB of HBM per device.

v0:
```python
import jax
import jax.numpy as jnp
from jax import lax
from jax.sharding import PartitionSpec as P


def inner(left, right):
    return lax.dot_general(
        left,
        right,
        (((1,), (1,)), ((), ())),
        precision=lax.Precision.HIGHEST,
        preferred_element_type=jnp.float32,
    )


def per_device(resident_x, resident_g, query_x, query_g):
    stacked = jnp.stack((query_x, query_g))
    piece = lax.all_gather(stacked, "tok", axis=1, tiled=True)
    partial_value = jnp.stack((inner(resident_x, piece[0]), inner(resident_g, piece[1])))
    sums = lax.psum_scatter(partial_value, "wid", scatter_dimension=1, tiled=True)
    return sums[0] * sums[1]


def solution(mesh):
    return jax.shard_map(
        per_device,
        mesh=mesh,
        in_specs=(P("tok", "wid"), P("tok", "wid"), P("tok", "wid"), P("tok", "wid")),
        out_specs=P(("tok", "wid"), None),
        check_vma=False,
    )
```

profile of v0, /device:TPU:0, one launch (start us, length us, event | category | flops | bytes accessed | tf_op | source)
XLA Modules:
  0.0 291.1 jit_solution(5934819000721754272)
XLA Ops:
  6.5 0.0 all-gather.2.cloned.1.call-start
  6.5 2.4 pad_maximum_fusion.1
  8.9 0.0 all-gather.2.cloned.1.call-update
  8.9 0.0 reduce-scatter.2.cloned.1.call-start
  9.0 112.1 %all-gather.2.cloned.1.call-done = f32[2,1024,1024]{2,1,0:T(8,128)} async-done(((f32[2,128,1024]{2,1,0:T(8,128)}), f32[2,1024,1024]{2,1,0:T(8,128)}) %all-gather.2.cloned.1.call-update) | async-done | bytes 8388624 | tf_op jit(solution)/shard_map/all_gather | solution.py:19
  121.1 0.0 copy-start
  121.1 29.8 %convolution_bitcast_fusion = f32[1,2048,1024]{1,2,0:T(8,128)S(1)} fusion(f32[2048,1024]{1,0:T(8,128)} %param.5, f32[2,1024,1024]{2,1,0:T(8,128)} %all-gather.2.cloned.1.call-done), kind=kOutput, calls=%fused_computation.1 | convolution fusion | flops 25769803776 | bytes 20971520 | tf_op jit(solution)/shard_map/dot_general | solution.py:8
  150.9 0.0 copy-done
  150.9 28.6 %convolution_bitcast_fusion.1 = f32[1,2048,1024]{1,2,0:T(8,128)S(1)} fusion(f32[2048,1024]{1,0:T(8,128)} %param.4, f32[2,1024,1024]{2,1,0:T(8,128)S(1)} %copy-done), kind=kOutput, calls=%fused_computation.2 | convolution fusion | flops 25769803776 | bytes 20971520 | tf_op jit(solution)/shard_map/dot_general | solution.py:8
  179.6 6.2 %pad_maximum_fusion = f32[2,2048,1024]{1,2,0:T(8,128)} fusion(f32[1,2048,1024]{1,2,0:T(8,128)S(1)} %convolution_bitcast_fusion, f32[1,2048,1024]{1,2,0:T(8,128)S(1)} %convolution_bitcast_fusion.1), kind=kLoop, calls=%fused_computation | loop fusion | flops 4194304 | bytes 33554432 | tf_op jit(solution)/shard_map/stack | solution.py:20
  185.8 0.0 reduce-scatter.2.cloned.1.call-update
  185.8 96.3 %reduce-scatter.2.cloned.1.call-done = f32[2,128,1024]{1,2,0:T(8,128)} async-done(((f32[2,2048,1024]{1,2,0:T(8,128)}), f32[2,128,1024]{1,2,0:T(8,128)}) %reduce-scatter.2.cloned.1.call-update) | async-done | bytes 1048592 | tf_op jit(solution)/shard_map/reduce_scatter | solution.py:21
  282.1 1.3 fusion
  283.3 1.0 copy.5
Async XLA Ops:
  6.5 114.5 %all-gather.2.cloned.1.call-start = ((), (), s32[]{:S(2)}) async-start(), calls=%async_computation.1 | async-start | bytes 9437184 | tf_op jit(solution)/shard_map/all_gather | solution.py:19
  8.9 273.1 %reduce-scatter.2.cloned.1.call-start = ((), (), s32[]{:S(2)}) async-start(), calls=%async_computation.2 | async-start | bytes 17825792 | tf_op jit(solution)/shard_map/reduce_scatter | solution.py:21
  121.1 29.8 %copy-start = (f32[2,1024,1024]{2,1,0:T(8,128)S(1)}, f32[2,1024,1024]{2,1,0:T(8,128)}, u32[]{:S(2)}) copy-start(f32[2,1024,1024]{2,1,0:T(8,128)} %all-gather.2.cloned.1.call-done) | copy-start | bytes 25165828
Sparse Core Ops, SparseCore 0:
  9.7 111.3 all-gather.1
  185.9 96.0 reduce-scatter.1
where the time goes:
time: 291 us
  waiting for transfers between devices  208 us (71%)
  matrix products  58.5 us (20%)
  between operations  13.4 us (5%)
  other arithmetic  9.82 us (3%)
    all_gather x1, waiting for transfers between devices, per_device(): piece = lax.all_gather(stacked, 'tok', axis=1, tiled=True)  112 us
    reduce_scatter x1, waiting for transfers between devices, per_device(): lax.psum_scatter(partial_value, 'wid', scatter_dimension=1, tiled=True)  96.3 us
    dot_general x2, matrix products, inner(): lax.dot_general(left, right, (((1,), (1,)), ((), ())), precision=lax.Prec...  58.5 us
    another operation x1, other arithmetic, per_device(): jnp.stack((inner(resident_x, piece[0]), inner(resident_g, piece[1])))  6.21 us
  transfers between devices with their start and end apart: 2, of which 2 were waited for; matrix products, arithmetic and copies ran while one was open for 0% of the time, Pallas kernels for 0%

commit v1 on v0

v1 whole, which is shorter than its diff:
```python
import functools

import jax
import jax.numpy as jnp
from jax import lax
from jax.experimental import pallas as pl
from jax.experimental.pallas import tpu as pltpu
from jax.sharding import PartitionSpec as P

MESH = pl.DeviceIdType.MESH
F32, BF16 = jnp.float32, jnp.bfloat16
NT = (((1,), (1,)), ((), ()))

BLOCKS = ((0, 1, 0, 0), (2, 5, 0, 1), (3, 6, 3, 0), (4, 7, 1, 0), (10, 11, 2, 0), (8, 12, 3, 1), (9, 13, 1, 1), (14, 15, 2, 1))
HALVED = (10, 11, 14, 15)
UNITS = 16
REL = (2, 1, 3, 0)
STAGES = 4


def kernel(rx, rg, qx, qg, out, rh, rl, qbuf, qcat, stage, pbuf, csum, y1, y2, zin,
           load_sem, stage_sem, ag_send, ag_recv, c_send, c_recv, y1_send, y1_recv, y2_send, y2_recv, z_send, z_recv):
    t, w = lax.axis_index("tok"), lax.axis_index("wid")
    zh, x = t // 4, t % 4
    zl, y, c = w // 8, (w // 2) % 4, w % 2
    right, left = (zh * 4 + (x + 1) % 4, w), (zh * 4 + (x + 3) % 4, w)
    partner = ((1 - zh) * 4 + x, w)
    up, down = (t, zl * 8 + ((y + 1) % 4) * 2 + c), (t, zl * 8 + ((y + 3) % 4) * 2 + c)
    sibling = (t, zl * 8 + y * 2 + 1 - c)
    across = (t, (1 - zl) * 8 + y * 2 + c)

    def remote(src, dst, send, recv, target):
        return pltpu.make_async_remote_copy(src_ref=src, dst_ref=dst, send_sem=send, recv_sem=recv, device_id=target, device_id_type=MESH)

    def gather(src, unit, half, target, sem):
        ref = {0: qx, 1: qg}.get(src, qbuf.at[src])
        rows = pl.ds(0, 128) if half is None else pl.ds(half * 64, 64)
        return remote(ref.at[rows], qbuf.at[unit, rows], ag_send.at[sem], ag_recv.at[unit, half or 0], target)

    own = [gather(0, 3, None, right, 0), gather(0, 4, None, left, 1), gather(0, 2, None, partner, 2),
           gather(1, 6, None, right, 3), gather(1, 7, None, left, 4), gather(1, 5, None, partner, 5)]
    forward = {
        2: [gather(2, 8, None, right, 6), gather(2, 9, None, left, 7)],
        3: [gather(3, 10, 0, right, 8)],
        4: [gather(4, 10, 1, left, 9)],
        6: [gather(6, 11, 0, right, 10), gather(6, 12, None, partner, 11)],
        7: [gather(7, 11, 1, left, 12), gather(7, 13, None, partner, 13)],
        8: [gather(8, 14, 0, right, 14)],
        9: [gather(9, 14, 1, left, 15)],
        12: [gather(12, 15, 0, right, 16)],
        13: [gather(13, 15, 1, left, 17)],
    }

    def load(matrix, s, half):
        row = pl.multiple_of(half * 1024 + ((y + REL[s]) % 4) * 256, 256)
        slot = (s * 2 + half) % STAGES
        return pltpu.make_async_copy((rx, rg)[matrix].at[pl.ds(row, 256)], stage.at[slot], stage_sem.at[slot])

    def split(matrix, s):
        for half in range(2):
            slot = (s * 2 + half) % STAGES
            load(matrix, s, half).wait()
            value = stage[slot]
            hi = value.astype(BF16)
            rh[matrix, s, pl.ds(half * 256, 256)] = hi
            rl[matrix, s, pl.ds(half * 256, 256)] = (value - hi.astype(F32)).astype(BF16)
            later = s * 2 + half + STAGES
            if matrix * 8 + later < 16:
                load(matrix + later // 8, (later % 8) // 2, half).start()

    barrier = pltpu.get_barrier_semaphore()
    others = (right, left, partner, up, down, sibling, across)
    for other in others:
        pl.semaphore_signal(barrier, inc=1, device_id=other, device_id_type=MESH)
    mine = [pltpu.make_async_copy(qx, qbuf.at[0], load_sem.at[0]), pltpu.make_async_copy(qg, qbuf.at[1], load_sem.at[1])]
    mine[0].start()
    for s in range(2):
        for half in range(2):
            load(0, s, half).start()
    mine[1].start()
    pl.semaphore_wait(barrier, len(others))
    for copy in own:
        copy.start()

    def core_copy(u, s):
        return remote(pbuf.at[s, 1 - c], csum.at[u, s], c_send.at[s], c_recv.at[u, s], sibling)

    def y1_copies(u):
        return (remote(csum.at[u, 0, 0], y1.at[u, 0], y1_send.at[u, 0], y1_recv.at[u, 0], up),
                remote(csum.at[u, 0, 1], y1.at[u, 1], y1_send.at[u, 1], y1_recv.at[u, 1], down))

    def y2_copies(u):
        return (remote(csum.at[u, 1], y2.at[u, 0], y2_send.at[u, 0], y2_recv.at[u, 0], up),
                remote(csum.at[u, 2], y2.at[u, 1], y2_send.at[u, 1], y2_recv.at[u, 1], down))

    def z_copy(u):
        return remote(csum.at[u, 3, 1 - zl], zin.at[u], z_send.at[u], z_recv.at[u], across)

    def arrive(k):
        if k < 2:
            mine[k].wait()
            return
        for half in (0, 1) if k in HALVED else (None,):
            gather(2, k, half, right, 0).wait_recv()
        for copy in forward.get(k, ()):
            copy.start()

    def core_stage(u, s):
        core_copy(u, s).wait_recv()
        csum[u, s] += pbuf[s, c]
        if s == 0:
            for copy in y1_copies(u):
                copy.start()

    def y1_stage(u):
        for i, (first, second) in enumerate(zip(y1_copies(u), y2_copies(u))):
            first.wait_recv()
            csum[u, 1 + i, i] += y1[u, i]
            second.start()

    def y2_stage(u):
        for copy in y2_copies(u):
            copy.wait_recv()
        csum[u, 3] += y2[u, 0] + y2[u, 1]
        z_copy(u).start()

    def unit(u, carry):
        matrix = ((u + 1) // 3 + 1 + u // 15 + (15 - u) // 15) % 2
        for k in range(UNITS):
            pl.when(u == k)(functools.partial(arrive, k))
        value = qbuf[u]
        hi = value.astype(BF16)
        qcat[pl.ds(0, 128)] = hi
        qcat[pl.ds(128, 128)] = (value - hi.astype(F32)).astype(BF16)
        for s in range(4):
            for k in range(2):
                pl.when(u == k)(functools.partial(split, k, s))

            @pl.when(u >= 1)
            def _():
                core_copy(u - 1, s).wait_send()

            q = qcat[...]
            product = lax.dot_general(rh[matrix, s], q, NT, preferred_element_type=F32)
            product += lax.dot_general(rl[matrix, s], q, NT, preferred_element_type=F32)
            product = product[:, :128] + product[:, 128:]
            for i in range(4):
                pbuf[s, i % 2, i // 2] = product[i * 128:(i + 1) * 128]
            core_copy(u, s).start()
            if s >= 2:
                core_stage(u, s - 2)
            else:
                pl.when(u >= 1)(functools.partial(core_stage, u - 1, s + 2))
            if s == 2:
                pl.when(u >= 1)(functools.partial(y1_stage, u - 1))
            if s == 0:
                pl.when(u >= 3)(functools.partial(y2_stage, u - 3))
        return carry

    lax.fori_loop(0, UNITS, unit, 0)
    last = UNITS - 1
    core_stage(last, 2)
    core_stage(last, 3)
    y1_stage(last)

    def gram(u):
        z_copy(u).wait_recv()
        return csum[u, 3, zl] + zin[u]

    def finish(block):
        first, second, dx, flip = block
        source = ((zh + flip) % 2) * 4 + (x + dx) % 4
        out[:, pl.ds(pl.multiple_of(source * 128, 128), 128)] = gram(first) * gram(second)

    y2_stage(last - 2)
    for block in BLOCKS[:6]:
        finish(block)
    y2_stage(last - 1)
    finish(BLOCKS[6])
    y2_stage(last)
    finish(BLOCKS[7])

    for copy in own + [copy for copies in forward.values() for copy in copies]:
        copy.wait_send()
    for s in range(4):
        core_copy(last, s).wait_send()

    def drain(u, carry):
        for copy in (*y1_copies(u), *y2_copies(u), z_copy(u)):
            copy.wait_send()
        return carry

    lax.fori_loop(0, UNITS, drain, 0)


def per_device(resident_x, resident_g, query_x, query_g):
    dma = pltpu.SemaphoreType.DMA
    return pl.pallas_call(
        kernel,
        out_shape=jax.ShapeDtypeStruct((128, 1024), F32),
        in_specs=[pl.BlockSpec(memory_space=pl.ANY)] * 4,
        out_specs=pl.BlockSpec(memory_space=pltpu.VMEM),
        scratch_shapes=[
            pltpu.VMEM((2, 4, 512, 1024), BF16),
            pltpu.VMEM((2, 4, 512, 1024), BF16),
            pltpu.VMEM((UNITS, 128, 1024), F32),
            pltpu.VMEM((256, 1024), BF16),
            pltpu.VMEM((STAGES, 256, 1024), F32),
            pltpu.VMEM((4, 2, 2, 128, 128), F32),
            pltpu.VMEM((UNITS, 4, 2, 128, 128), F32),
            pltpu.VMEM((UNITS, 2, 128, 128), F32),
            pltpu.VMEM((UNITS, 2, 2, 128, 128), F32),
            pltpu.VMEM((UNITS, 128, 128), F32),
            dma((2,)), dma((STAGES,)), dma((18,)), dma((UNITS, 2)), dma((4,)), dma((UNITS, 4)),
            dma((UNITS, 2)), dma((UNITS, 2)), dma((UNITS, 2)), dma((UNITS, 2)), dma((UNITS,)), dma((UNITS,)),
        ],
        compiler_params=pltpu.CompilerParams(collective_id=0, has_side_effects=True, vmem_limit_bytes=58 * 2**20),
    )(resident_x, resident_g, query_x, query_g)


def solution(mesh):
    return jax.shard_map(
        per_device,
        mesh=mesh,
        in_specs=(P("tok", "wid"), P("tok", "wid"), P("tok", "wid"), P("tok", "wid")),
        out_specs=P(("tok", "wid"), None),
        check_vma=False,
    )
```

time: 291 us -> 113 us (0.39)
  waiting for transfers between devices: 208 us -> 0 us
  Pallas kernels: 0 us -> 111 us
  matrix products: 58.5 us -> 0 us
  between operations: 13.4 us -> 0.01 us
  other arithmetic: 9.82 us -> 0 us
    all_gather x1 -> x0, waiting for transfers between devices: 112 us -> none  [per_device(): piece = lax.all_gather(stacked, 'tok', axis=1, tiled=True)]
    pallas_call x0 -> x1, Pallas kernels: none -> 111 us  [per_device(): pl.pallas_call(kernel, out_shape=jax.ShapeDtypeStruct((128, 1024), F32),...]
    reduce_scatter x1 -> x0, waiting for transfers between devices: 96.3 us -> none  [per_device(): lax.psum_scatter(partial_value, 'wid', scatter_dimension=1, tiled=True)]
    dot_general x2 -> x0, matrix products: 58.5 us -> none  [inner(): lax.dot_general(left, right, (((1,), (1,)), ((), ())), precision=lax.Prec...]
    another operation x2 -> x0, other arithmetic: 8.57 us -> none  [the longest x1 6.21 us: per_device(): jnp.stack((inner(resident_x, piece[0]), inner(resident_g, piece[1])))]
  transfers between devices with their start and end apart: 2 -> 0, of which waited for: 2 -> 0; matrix products, arithmetic and copies ran while one was open for 0% -> 0% of each run, Pallas kernels for 0% -> 0%
where the time goes in v1:
time: 113 us
  Pallas kernels  111 us (98%)
  local copies, waits for them, and re-layouts  1.89 us (2%)
    pallas_call x1, Pallas kernels, per_device(): pl.pallas_call(kernel, out_shape=jax.ShapeDtypeStruct((128, 1024), F32),...  111 us

profile of v1, /device:TPU:0, one launch (start us, length us, event | category | flops | bytes accessed | tf_op | source)
XLA Modules:
  0.0 112.6 jit_solution(6787894594311862344)
XLA Ops:
  0.0 110.7 %shard_map.46 = f32[128,1024]{1,0:T(8,128)} custom-call(f32[2048,1024]{1,0:T(8,128)} %rx.1, f32[2048,1024]{1,0:T(8,128)} %rg.1, f32[128,1024]{1,0:T(8,128)} %qx.1, f32[128,1024]{1,0:T(8,128)} %qg.1), custom_call_target="tpu_custom_call" | custom-call | tf_op jit(solution)/shard_map/pallas_call | solution.py:198
  110.7 1.9 %copy.6 = f32[128,1024]{1,0:T(8,128)} copy(f32[128,1024]{1,0:T(8,128)} %shard_map.46) | data formatting | bytes 1048576

commit v2 on v1

v2 whole, which is shorter than its diff:
```python
import functools

import jax
import jax.numpy as jnp
from jax import lax
from jax.experimental import pallas as pl
from jax.experimental.pallas import tpu as pltpu
from jax.sharding import PartitionSpec as P

MESH = pl.DeviceIdType.MESH
F32, BF16 = jnp.float32, jnp.bfloat16
NT = (((1,), (1,)), ((), ()))

BLOCKS = ((0, 1, 0, 0), (4, 7, 0, 1), (8, 11, 2, 0), (9, 12, 3, 1), (10, 13, 1, 1), (14, 15, 2, 1))
EAGER = 4
UNITS = 16
REL = (2, 1, 3, 0)
STAGES = 8
PARTS = ((0, 1), (1, 3), (3, 4))


def kernel(rx, rg, qx, qg, out, rh, rl, qbuf, qcat, stage, pbuf, csum, y1, y2, zin,
           load_sem, stage_sem, ag_send, ag_recv, c_send, c_recv, y1_send, y1_recv, y2_send, y2_recv, z_send, z_recv):
    t, w = lax.axis_index("tok"), lax.axis_index("wid")
    zh, x = t // 4, t % 4
    zl, y, c = w // 8, (w // 2) % 4, w % 2
    right, left = (zh * 4 + (x + 1) % 4, w), (zh * 4 + (x + 3) % 4, w)
    partner = ((1 - zh) * 4 + x, w)
    up, down = (t, zl * 8 + ((y + 1) % 4) * 2 + c), (t, zl * 8 + ((y + 3) % 4) * 2 + c)
    sibling = (t, zl * 8 + y * 2 + 1 - c)
    across = (t, (1 - zl) * 8 + y * 2 + c)

    def remote(src, dst, send, recv, target):
        return pltpu.make_async_remote_copy(src_ref=src, dst_ref=dst, send_sem=send, recv_sem=recv, device_id=target, device_id_type=MESH)

    def gather(src, start, unit, row, rows, target):
        ref = {0: qx, 1: qg}.get(src, qbuf.at[src])
        return remote(ref.at[pl.ds(start, rows)], qbuf.at[unit, pl.ds(row, rows)], ag_send, ag_recv.at[unit], target)

    own = []
    for m in range(2):
        own += [gather(m, 0, 2 + 3 * m, 0, 64, right), gather(m, 0, 2 + 3 * m, 64, 64, left), gather(m, 0, 4 + 3 * m, 0, 128, partner),
                gather(m, 64, 3 + 3 * m, 0, 64, right), gather(m, 64, 3 + 3 * m, 64, 64, left)]
    forward = {
        2: [gather(2, 0, 8, 0, 64, right)],
        3: [gather(3, 64, 8, 64, 64, left)],
        4: [gather(4, 0, 9, 0, 128, right), gather(4, 0, 10, 0, 128, left)],
        5: [gather(5, 0, 12, 0, 64, partner), gather(5, 64, 13, 0, 64, partner), gather(5, 0, 11, 0, 64, right)],
        6: [gather(6, 0, 12, 64, 64, partner), gather(6, 64, 13, 64, 64, partner), gather(6, 64, 11, 64, 64, left)],
        9: [gather(9, 0, 14, 0, 64, right)],
        10: [gather(10, 64, 14, 64, 64, left)],
        12: [gather(12, 0, 15, 0, 64, right)],
        13: [gather(13, 64, 15, 64, 64, left)],
    }

    def load(matrix, s, half):
        row = pl.multiple_of(half * 1024 + ((y + REL[s]) % 4) * 256, 256)
        slot = (s * 2 + half) % STAGES
        return pltpu.make_async_copy((rx, rg)[matrix].at[pl.ds(row, 256)], stage.at[slot], stage_sem.at[slot])

    def split(matrix, s):
        for half in range(2):
            slot = (s * 2 + half) % STAGES
            load(matrix, s, half).wait()
            value = stage[slot]
            hi = value.astype(BF16)
            rh[matrix, s, pl.ds(half * 256, 256)] = hi
            rl[matrix, s, pl.ds(half * 256, 256)] = (value - hi.astype(F32)).astype(BF16)
            if matrix == 0:
                load(1, s, half).start()

    barrier = pltpu.get_barrier_semaphore()
    others = (right, left, partner, up, down, sibling, across)
    for other in others:
        pl.semaphore_signal(barrier, inc=1, device_id=other, device_id_type=MESH)
    mine = [pltpu.make_async_copy(qx, qbuf.at[0], load_sem.at[0]), pltpu.make_async_copy(qg, qbuf.at[1], load_sem.at[1])]
    mine[0].start()
    for s in range(4):
        for half in range(2):
            load(0, s, half).start()
    mine[1].start()

    def core_copy(u, lo, hi):
        parts, part = pl.ds(lo, hi - lo), (lo + 1) // 2
        return remote(pbuf.at[u % 2, 1 - c, parts], csum.at[u, parts], c_send.at[u % 2, part], c_recv.at[UNITS + 2 * u + part - 1 if part else u], sibling)

    def y1_copies(u):
        return (remote(csum.at[u, 0, 0], y1.at[u, 0], y1_send, y1_recv.at[u], up),
                remote(csum.at[u, 0, 1], y1.at[u, 1], y1_send, y1_recv.at[u], down))

    def y2_copies(u):
        return (remote(csum.at[u, 1], y2.at[u, 0], y2_send, y2_recv.at[u], up),
                remote(csum.at[u, 2], y2.at[u, 1], y2_send, y2_recv.at[u], down))

    def z_copy(u):
        return remote(csum.at[u, 3, 1 - zl], zin.at[u], z_send, z_recv.at[u], across)

    def arrive(k):
        remote(qbuf.at[k], qbuf.at[k], ag_send, ag_recv.at[k], right).wait_recv()
        for copy in forward.get(k, ()):
            copy.start()

    def core_stage(u, lo, hi):
        core_copy(u, lo, hi).wait_recv()
        for s in range(lo, hi):
            csum[u, s] += pbuf[u % 2, c, s]
            if s == 0:
                for copy in y1_copies(u):
                    copy.start()

    def y1_stage(u):
        remote(y1.at[u], y1.at[u], y1_send, y1_recv.at[u], up).wait_recv()
        for i, copy in enumerate(y2_copies(u)):
            csum[u, 1 + i, i] += y1[u, i]
            copy.start()

    def y2_stage(u):
        remote(y2.at[u], y2.at[u], y2_send, y2_recv.at[u], up).wait_recv()
        csum[u, 3] += y2[u, 0] + y2[u, 1]
        z_copy(u).start()

    def queries(u, slot):
        value = qbuf[u]
        hi = value.astype(BF16)
        qcat[slot, pl.ds(0, 128)] = hi
        qcat[slot, pl.ds(128, 128)] = (value - hi.astype(F32)).astype(BF16)

    def dots(u, matrix, lo, hi):
        q = qcat[u if isinstance(u, int) else 0]
        for s in range(lo, hi):
            product = lax.dot_general(rh[matrix, s], q, NT, preferred_element_type=F32)
            product += lax.dot_general(rl[matrix, s], q, NT, preferred_element_type=F32)
            product = product[:, :128] + product[:, 128:]
            for i in range(4):
                pbuf[u % 2, i % 2, s, i // 2] = product[i * 128:(i + 1) * 128]

    def send(u, lo, hi):
        core_copy(u, lo, hi).start()

    mine[0].wait()
    queries(0, 0)
    split(0, 0)
    dots(0, 0, 0, 1)
    pl.semaphore_wait(barrier, len(others))
    send(0, 0, 1)
    for copy in own:
        copy.start()
    split(0, 1)
    split(0, 2)
    core_stage(0, 0, 1)
    dots(0, 0, 1, 3)
    send(0, 1, 3)
    mine[1].wait()
    queries(1, 1)
    split(1, 0)
    split(0, 3)
    core_stage(0, 1, 3)
    y1_stage(0)
    dots(1, 1, 0, 1)
    send(1, 0, 1)
    dots(0, 0, 3, 4)
    send(0, 3, 4)
    core_stage(1, 0, 1)
    split(1, 1)
    split(1, 2)
    dots(1, 1, 1, 3)
    send(1, 1, 3)
    split(1, 3)
    core_stage(0, 3, 4)
    core_stage(1, 1, 3)
    y1_stage(1)
    dots(1, 1, 3, 4)
    send(1, 3, 4)
    for lo, hi in PARTS:
        core_copy(0, lo, hi).wait_send()

    def stages(u):
        @pl.when(u >= 3)
        def _():
            core_stage(u - 1, 0, 4)
            core_copy(u - 1, 0, 4).wait_send()

        @pl.when(u >= 4)
        def _():
            y1_stage(u - 2)

    def unit(u, carry):
        matrix = ((u + 1) // 3 + 1 + u // 15) % 2
        pl.when(u <= EAGER)(functools.partial(stages, u))
        for k in range(2, UNITS):
            pl.when(u == k)(functools.partial(arrive, k))
        queries(u, 0)
        dots(u, matrix, 0, 4)
        send(u, 0, 4)

        @pl.when(u == 2)
        def _():
            core_stage(1, 3, 4)
            for lo, hi in PARTS:
                core_copy(1, lo, hi).wait_send()

        pl.when(u > EAGER)(functools.partial(stages, u))

        @pl.when((u >= 9) & (u < 14))
        def _():
            y2_stage(2 * (u - 9))
            y2_stage(2 * (u - 9) + 1)

        @pl.when(u >= 14)
        def _():
            y2_stage(u - 4)

        return carry

    lax.fori_loop(2, UNITS, unit, 0)
    last = UNITS - 1
    core_stage(last, 0, 4)
    y1_stage(last - 1)
    y2_stage(last - 3)
    y1_stage(last)

    def gram(u):
        z_copy(u).wait_recv()
        return csum[u, 3, zl] + zin[u]

    def store(dx, flip, value):
        source = ((zh + flip) % 2) * 4 + (x + dx) % 4
        out[:, pl.ds(pl.multiple_of(source * 128, 128), 128)] = value

    def finish(block):
        first, second, dx, flip = block
        store(dx, flip, gram(first) * gram(second))

    y2_stage(last - 2)
    halves = gram(2) * gram(5), gram(3) * gram(6)
    store(3, 0, jnp.concatenate([half[:, :64] for half in halves], axis=1))
    store(1, 0, jnp.concatenate([half[:, 64:] for half in halves], axis=1))
    for block in BLOCKS[:4]:
        finish(block)
    y2_stage(last - 1)
    finish(BLOCKS[4])
    y2_stage(last)
    finish(BLOCKS[5])

    core_copy(last, 0, 4).wait_send()
    everything = qbuf.at[pl.ds(2, UNITS - 2)]
    for ref, sem in ((everything, ag_send), (y1, y1_send), (y2, y2_send), (zin, z_send)):
        remote(ref, ref, sem, sem, right).wait_send()


def per_device(resident_x, resident_g, query_x, query_g):
    dma = pltpu.SemaphoreType.DMA
    return pl.pallas_call(
        kernel,
        out_shape=jax.ShapeDtypeStruct((128, 1024), F32),
        in_specs=[pl.BlockSpec(memory_space=pl.ANY)] * 4,
        out_specs=pl.BlockSpec(memory_space=pltpu.VMEM),
        scratch_shapes=[
            pltpu.VMEM((2, 4, 512, 1024), BF16),
            pltpu.VMEM((2, 4, 512, 1024), BF16),
            pltpu.VMEM((UNITS, 128, 1024), F32),
            pltpu.VMEM((2, 256, 1024), BF16),
            pltpu.VMEM((STAGES, 256, 1024), F32),
            pltpu.VMEM((2, 2, 4, 2, 128, 128), F32),
            pltpu.VMEM((UNITS, 4, 2, 128, 128), F32),
            pltpu.VMEM((UNITS, 2, 128, 128), F32),
            pltpu.VMEM((UNITS, 2, 2, 128, 128), F32),
            pltpu.VMEM((UNITS, 128, 128), F32),
            dma((2,)), dma((STAGES,)), dma, dma((UNITS,)), dma((2, 3)), dma((UNITS + 4,)),
            dma, dma((UNITS,)), dma, dma((UNITS,)), dma, dma((UNITS,)),
        ],
        compiler_params=pltpu.CompilerParams(collective_id=0, has_side_effects=True, vmem_limit_bytes=58 * 2**20),
    )(resident_x, resident_g, query_x, query_g)


def solution(mesh):
    return jax.shard_map(
        per_device,
        mesh=mesh,
        in_specs=(P("tok", "wid"), P("tok", "wid"), P("tok", "wid"), P("tok", "wid")),
        out_specs=P(("tok", "wid"), None),
        check_vma=False,
    )
```

time: 113 us -> 97.6 us (0.86)
  Pallas kernels: 111 us -> 95.6 us
    pallas_call x1, Pallas kernels: 111 us -> 95.6 us  [per_device(): pl.pallas_call(kernel, out_shape=jax.ShapeDtypeStruct((128, 1024), F32),...]
where the time goes in v2:
time: 97.6 us; the launch traced here: 97.5 us
  Pallas kernels  95.6 us (98%)
  local copies, waits for them, and re-layouts  1.89 us (2%)
    pallas_call x1, Pallas kernels, per_device(): pl.pallas_call(kernel, out_shape=jax.ShapeDtypeStruct((128, 1024), F32),...  95.6 us

profile of v2, /device:TPU:0, one launch (start us, length us, event | category | flops | bytes accessed | tf_op | source)
XLA Modules:
  0.0 97.5 jit_solution(5013069100556504496)
XLA Ops:
  0.0 95.6 %shard_map.46 = f32[128,1024]{1,0:T(8,128)} custom-call(f32[2048,1024]{1,0:T(8,128)} %rx.1, f32[2048,1024]{1,0:T(8,128)} %rg.1, f32[128,1024]{1,0:T(8,128)} %qx.1, f32[128,1024]{1,0:T(8,128)} %qg.1), custom_call_target="tpu_custom_call" | custom-call | tf_op jit(solution)/shard_map/pallas_call | solution.py:253
  95.6 1.9 %copy.6 = f32[128,1024]{1,0:T(8,128)} copy(f32[128,1024]{1,0:T(8,128)} %shard_map.46) | data formatting | bytes 1048576

commit v3 on v2

--- a/solution.py
+++ b/solution.py
@@ -12,15 +12,17 @@
 NT = (((1,), (1,)), ((), ()))
 
 BLOCKS = ((0, 1, 0, 0), (4, 7, 0, 1), (8, 11, 2, 0), (9, 12, 3, 1), (10, 13, 1, 1), (14, 15, 2, 1))
-EAGER = 4
+ACROSS_FIRST = (11, 13)
+STEPS = ("CyAY", "ACyZW", "yACy", "ACZW", "yACyZ", "ACyW", "ACYCZZZ", "YCAYW", "YAYW", "CyAyC", "AyC", "ACY", "ACYZ", "yAyC")
+LAST = "ZCWYWZZYZYZYZZZZZ"
 UNITS = 16
 REL = (2, 1, 3, 0)
-STAGES = 8
+STAGES = 16
 PARTS = ((0, 1), (1, 3), (3, 4))
 
 
-def kernel(rx, rg, qx, qg, out, rh, rl, qbuf, qcat, stage, pbuf, csum, y1, y2, zin,
-           load_sem, stage_sem, ag_send, ag_recv, c_send, c_recv, y1_send, y1_recv, y2_send, y2_recv, z_send, z_recv):
+def kernel(rx, rg, qx, qg, out, rh, rl, qbuf, qcat, stage, pbuf, csum, y1, y2, zin, zfirst,
+           load_sem, stage_sem, ag_send, ag_recv, c_send, c_recv, y1_send, y1_recv, y2_send, y2_recv, z_send, z_recv, first_send, first_recv):
     t, w = lax.axis_index("tok"), lax.axis_index("wid")
     zh, x = t // 4, t % 4
     zl, y, c = w // 8, (w // 2) % 4, w % 2
@@ -55,19 +57,19 @@
 
     def load(matrix, s, half):
         row = pl.multiple_of(half * 1024 + ((y + REL[s]) % 4) * 256, 256)
-        slot = (s * 2 + half) % STAGES
+        slot = matrix * 8 + s * 2 + half
         return pltpu.make_async_copy((rx, rg)[matrix].at[pl.ds(row, 256)], stage.at[slot], stage_sem.at[slot])
 
-    def split(matrix, s):
-        for half in range(2):
-            slot = (s * 2 + half) % STAGES
-            load(matrix, s, half).wait()
-            value = stage[slot]
-            hi = value.astype(BF16)
-            rh[matrix, s, pl.ds(half * 256, 256)] = hi
-            rl[matrix, s, pl.ds(half * 256, 256)] = (value - hi.astype(F32)).astype(BF16)
-            if matrix == 0:
-                load(1, s, half).start()
+    def split(matrix, *parts):
+        for s in parts:
+            for half in range(2):
+                load(matrix, s, half).wait()
+        for s in parts:
+            for half in range(2):
+                value = stage[matrix * 8 + s * 2 + half]
+                hi = value.astype(BF16)
+                rh[matrix, s, pl.ds(half * 256, 256)] = hi
+                rl[matrix, s, pl.ds(half * 256, 256)] = (value - hi.astype(F32)).astype(BF16)
 
     barrier = pltpu.get_barrier_semaphore()
     others = (right, left, partner, up, down, sibling, across)
@@ -75,9 +77,9 @@
         pl.semaphore_signal(barrier, inc=1, device_id=other, device_id_type=MESH)
     mine = [pltpu.make_async_copy(qx, qbuf.at[0], load_sem.at[0]), pltpu.make_async_copy(qg, qbuf.at[1], load_sem.at[1])]
     mine[0].start()
-    for s in range(4):
+    for matrix, s in ((0, 0), (0, 1), (0, 2), (1, 0), (0, 3), (1, 1), (1, 2), (1, 3)):
         for half in range(2):
-            load(0, s, half).start()
+            load(matrix, s, half).start()
     mine[1].start()
 
     def core_copy(u, lo, hi):
@@ -85,15 +87,26 @@
         return remote(pbuf.at[u % 2, 1 - c, parts], csum.at[u, parts], c_send.at[u % 2, part], c_recv.at[UNITS + 2 * u + part - 1 if part else u], sibling)
 
     def y1_copies(u):
+        if u in ACROSS_FIRST:
+            low, high = pl.ds(0, 64), pl.ds(64, 64)
+            return (remote(csum.at[u, 0, zl, low], y1.at[u, 0, low], y1_send, y1_recv.at[u], up),
+                    remote(csum.at[u, 0, zl, high], y1.at[u, 1, high], y1_send, y1_recv.at[u], down))
         return (remote(csum.at[u, 0, 0], y1.at[u, 0], y1_send, y1_recv.at[u], up),
                 remote(csum.at[u, 0, 1], y1.at[u, 1], y1_send, y1_recv.at[u], down))
 
     def y2_copies(u):
+        if u in ACROSS_FIRST:
+            return (remote(csum.at[u, 1, zl], y2.at[u, 0, 0], y2_send, y2_recv.at[u], up),
+                    remote(csum.at[u, 2, zl], y2.at[u, 1, 0], y2_send, y2_recv.at[u], down))
         return (remote(csum.at[u, 1], y2.at[u, 0], y2_send, y2_recv.at[u], up),
                 remote(csum.at[u, 2], y2.at[u, 1], y2_send, y2_recv.at[u], down))
 
     def z_copy(u):
         return remote(csum.at[u, 3, 1 - zl], zin.at[u], z_send, z_recv.at[u], across)
+
+    def first_copy(u):
+        i = ACROSS_FIRST.index(u)
+        return remote(csum.at[u, :, 1 - zl], zfirst.at[i], first_send, first_recv.at[i], across)
 
     def arrive(k):
         remote(qbuf.at[k], qbuf.at[k], ag_send, ag_recv.at[k], right).wait_recv()
@@ -104,20 +117,41 @@
         core_copy(u, lo, hi).wait_recv()
         for s in range(lo, hi):
             csum[u, s] += pbuf[u % 2, c, s]
+            if s == 0 and u not in ACROSS_FIRST:
+                for copy in y1_copies(u):
+                    copy.start()
+        if u in ACROSS_FIRST:
+            first_copy(u).start()
+
+    def across_stage(u):
+        first_copy(u).wait_recv()
+        for s in range(4):
+            csum[u, s, zl] += zfirst[ACROSS_FIRST.index(u), s]
             if s == 0:
                 for copy in y1_copies(u):
                     copy.start()
 
     def y1_stage(u):
-        remote(y1.at[u], y1.at[u], y1_send, y1_recv.at[u], up).wait_recv()
+        half = u in ACROSS_FIRST
+        landed = y1.at[u, :, pl.ds(0, 64)] if half else y1.at[u]
+        remote(landed, landed, y1_send, y1_recv.at[u], up).wait_recv()
         for i, copy in enumerate(y2_copies(u)):
-            csum[u, 1 + i, i] += y1[u, i]
+            if half:
+                rows = pl.ds(i * 64, 64)
+                csum[u, 1 + i, zl, rows] += y1[u, i, rows]
+            else:
+                csum[u, 1 + i, i] += y1[u, i]
             copy.start()
 
     def y2_stage(u):
-        remote(y2.at[u], y2.at[u], y2_send, y2_recv.at[u], up).wait_recv()
-        csum[u, 3] += y2[u, 0] + y2[u, 1]
-        z_copy(u).start()
+        half = u in ACROSS_FIRST
+        landed = y2.at[u, :, 0] if half else y2.at[u]
+        remote(landed, landed, y2_send, y2_recv.at[u], up).wait_recv()
+        if half:
+            csum[u, 3, zl] += y2[u, 0, 0] + y2[u, 1, 0]
+        else:
+            csum[u, 3] += y2[u, 0] + y2[u, 1]
+            z_copy(u).start()
 
     def queries(u, slot):
         value = qbuf[u]
@@ -145,81 +179,96 @@
     send(0, 0, 1)
     for copy in own:
         copy.start()
-    split(0, 1)
-    split(0, 2)
+    mine[1].wait()
+    queries(1, 1)
+    split(0, 1, 2)
+    split(1, 0)
     core_stage(0, 0, 1)
+    dots(1, 1, 0, 1)
+    send(1, 0, 1)
     dots(0, 0, 1, 3)
     send(0, 1, 3)
-    mine[1].wait()
-    queries(1, 1)
-    split(1, 0)
-    split(0, 3)
+    core_stage(1, 0, 1)
+    split(1, 1, 2)
     core_stage(0, 1, 3)
     y1_stage(0)
-    dots(1, 1, 0, 1)
-    send(1, 0, 1)
+    dots(1, 1, 1, 3)
+    send(1, 1, 3)
+    split(0, 3)
+    split(1, 3)
     dots(0, 0, 3, 4)
     send(0, 3, 4)
-    core_stage(1, 0, 1)
-    split(1, 1)
-    split(1, 2)
-    dots(1, 1, 1, 3)
-    send(1, 1, 3)
-    split(1, 3)
-    core_stage(0, 3, 4)
     core_stage(1, 1, 3)
     y1_stage(1)
-    dots(1, 1, 3, 4)
-    send(1, 3, 4)
-    for lo, hi in PARTS:
-        core_copy(0, lo, hi).wait_send()
-
-    def stages(u):
-        @pl.when(u >= 3)
-        def _():
-            core_stage(u - 1, 0, 4)
-            core_copy(u - 1, 0, 4).wait_send()
-
-        @pl.when(u >= 4)
-        def _():
-            y1_stage(u - 2)
+
+    summed, on_y1, on_y2, on_z = 1, [], [0, 1], []
+    done = []
+
+    def plan(steps):
+        nonlocal summed
+        todo = []
+        for step in steps:
+            if step == "C" and summed < ready:
+                summed += 1
+                todo.append((core_stage, summed, 0, 4))
+                (on_z if summed in ACROSS_FIRST else on_y1).append(summed)
+            elif step == "W" and on_z:
+                todo.append((across_stage, on_z[0]))
+                on_y1.append(on_z.pop(0))
+            elif step in "Yy" and len(on_y1) > (step == "y"):
+                todo.append((y1_stage, on_y1[0]))
+                on_y2.append(on_y1.pop(0))
+            elif step == "Z" and on_y2:
+                todo.append((y2_stage, on_y2[0]))
+                done.append(on_y2.pop(0))
+        return todo
+
+    before, after = {}, {}
+    for k in range(2, UNITS):
+        ready = k - 1
+        first, second = STEPS[k - 2].split("A")
+        before[k] = plan(first)
+        assert summed >= k - 2
+        ready = k
+        after[k] = plan(second)
+    ending = plan(LAST + "CC" + "WYWY" + "Y" * UNITS + "Z" * UNITS)
+
+    def carry_out(todo):
+        for stage_of, *which in todo:
+            stage_of(*which)
+
+    def begin(k):
+        if k < 4:
+            core_stage(k - 2, 3, 4)
+        carry_out(before[k])
+        arrive(k)
+        for lo, hi in PARTS if k < 4 else ((0, 4),):
+            core_copy(k - 2, lo, hi).wait_send()
+
+    def end(k):
+        if k == 2:
+            dots(1, 1, 3, 4)
+            send(1, 3, 4)
+        carry_out(after[k])
 
     def unit(u, carry):
         matrix = ((u + 1) // 3 + 1 + u // 15) % 2
-        pl.when(u <= EAGER)(functools.partial(stages, u))
         for k in range(2, UNITS):
-            pl.when(u == k)(functools.partial(arrive, k))
+            pl.when(u == k)(functools.partial(begin, k))
         queries(u, 0)
         dots(u, matrix, 0, 4)
         send(u, 0, 4)
-
-        @pl.when(u == 2)
-        def _():
-            core_stage(1, 3, 4)
-            for lo, hi in PARTS:
-                core_copy(1, lo, hi).wait_send()
-
-        pl.when(u > EAGER)(functools.partial(stages, u))
-
-        @pl.when((u >= 9) & (u < 14))
-        def _():
-            y2_stage(2 * (u - 9))
-            y2_stage(2 * (u - 9) + 1)
-
-        @pl.when(u >= 14)
-        def _():
-            y2_stage(u - 4)
-
+        for k in range(2, UNITS):
+            pl.when(u == k)(functools.partial(end, k))
         return carry
 
     lax.fori_loop(2, UNITS, unit, 0)
     last = UNITS - 1
-    core_stage(last, 0, 4)
-    y1_stage(last - 1)
-    y2_stage(last - 3)
-    y1_stage(last)
+    carry_out(ending)
 
     def gram(u):
+        if u in ACROSS_FIRST:
+            return csum[u, 3, zl]
         z_copy(u).wait_recv()
         return csum[u, 3, zl] + zin[u]
 
@@ -231,20 +280,17 @@
         first, second, dx, flip = block
         store(dx, flip, gram(first) * gram(second))
 
-    y2_stage(last - 2)
     halves = gram(2) * gram(5), gram(3) * gram(6)
     store(3, 0, jnp.concatenate([half[:, :64] for half in halves], axis=1))
     store(1, 0, jnp.concatenate([half[:, 64:] for half in halves], axis=1))
-    for block in BLOCKS[:4]:
+    for block in sorted(BLOCKS, key=lambda block: max(done.index(u) for u in block[:2])):
         finish(block)
-    y2_stage(last - 1)
-    finish(BLOCKS[4])
-    y2_stage(last)
-    finish(BLOCKS[5])
-
-    core_copy(last, 0, 4).wait_send()
-    everything = qbuf.at[pl.ds(2, UNITS - 2)]
-    for ref, sem in ((everything, ag_send), (y1, y1_send), (y2, y2_send), (zin, z_send)):
+
+    for u in (last - 1, last):
+        core_copy(u, 0, 4).wait_send()
+    whole = pl.ds(0, UNITS - len(ACROSS_FIRST) // 2)
+    for ref, sem in ((qbuf.at[pl.ds(2, UNITS - 2)], ag_send), (y1.at[whole], y1_send), (y2.at[whole], y2_send),
+                     (zin.at[pl.ds(0, UNITS - len(ACROSS_FIRST))], z_send), (zfirst, first_send)):
         remote(ref, ref, sem, sem, right).wait_send()
 
 
@@ -266,10 +312,11 @@
             pltpu.VMEM((UNITS, 2, 128, 128), F32),
             pltpu.VMEM((UNITS, 2, 2, 128, 128), F32),
             pltpu.VMEM((UNITS, 128, 128), F32),
+            pltpu.VMEM((len(ACROSS_FIRST), 4, 128, 128), F32),
             dma((2,)), dma((STAGES,)), dma, dma((UNITS,)), dma((2, 3)), dma((UNITS + 4,)),
-            dma, dma((UNITS,)), dma, dma((UNITS,)), dma, dma((UNITS,)),
+            dma, dma((UNITS,)), dma, dma((UNITS,)), dma, dma((UNITS,)), dma, dma((len(ACROSS_FIRST),)),
         ],
-        compiler_params=pltpu.CompilerParams(collective_id=0, has_side_effects=True, vmem_limit_bytes=58 * 2**20),
+        compiler_params=pltpu.CompilerParams(collective_id=0, has_side_effects=True, vmem_limit_bytes=61 * 2**20),
     )(resident_x, resident_g, query_x, query_g)
 
 

time: 97.6 us -> 93.4 us (0.957)
  Pallas kernels: 95.6 us -> 91.3 us
    pallas_call x1, Pallas kernels: 95.6 us -> 91.3 us  [per_device(): pl.pallas_call(kernel, out_shape=jax.ShapeDtypeStruct((128, 1024), F32),...]
where the time goes in v3:
time: 93.4 us; the launch traced here: 93.2 us
  Pallas kernels  91.3 us (98%)
  local copies, waits for them, and re-layouts  1.89 us (2%)
    pallas_call x1, Pallas kernels, per_device(): pl.pallas_call(kernel, out_shape=jax.ShapeDtypeStruct((128, 1024), F32),...  91.3 us
    unnamed x1, local copies, waits for them, and re-layouts  1.89 us

profile of v3, /device:TPU:0, one launch (start us, length us, event | category | flops | bytes accessed | tf_op | source)
XLA Modules:
  0.0 93.2 jit_solution(10083305313247123089)
XLA Ops:
  0.0 91.3 %shard_map.46 = f32[128,1024]{1,0:T(8,128)} custom-call(f32[2048,1024]{1,0:T(8,128)} %rx.1, f32[2048,1024]{1,0:T(8,128)} %rg.1, f32[128,1024]{1,0:T(8,128)} %qx.1, f32[128,1024]{1,0:T(8,128)} %qg.1), custom_call_target="tpu_custom_call" | custom-call | tf_op jit(solution)/shard_map/pallas_call | solution.py:299
  91.3 1.9 %copy.6 = f32[128,1024]{1,0:T(8,128)} copy(f32[128,1024]{1,0:T(8,128)} %shard_map.46) | data formatting | bytes 1048576

commit v4 on v3

--- a/solution.py
+++ b/solution.py
@@ -80,7 +80,8 @@
     for matrix, s in ((0, 0), (0, 1), (0, 2), (1, 0), (0, 3), (1, 1), (1, 2), (1, 3)):
         for half in range(2):
             load(matrix, s, half).start()
-    mine[1].start()
+        if (matrix, s) == (0, 0):
+            mine[1].start()
 
     def core_copy(u, lo, hi):
         parts, part = pl.ds(lo, hi - lo), (lo + 1) // 2

time: 93.4 us -> 93.4 us (level)
  no operation moved by 1% of the time
where the time goes in v4:
time: 93.4 us; the launch traced here: 93.2 us
  Pallas kernels  91.3 us (98%)
  local copies, waits for them, and re-layouts  1.89 us (2%)
    pallas_call x1, Pallas kernels, per_device(): pl.pallas_call(kernel, out_shape=jax.ShapeDtypeStruct((128, 1024), F32),...  91.3 us
    unnamed x1, local copies, waits for them, and re-layouts  1.89 us

profile of v4, /device:TPU:0, one launch (start us, length us, event | category | flops | bytes accessed | tf_op | source)
XLA Modules:
  0.0 93.2 jit_solution(16231946408182828751)
XLA Ops:
  0.0 91.3 %shard_map.46 = f32[128,1024]{1,0:T(8,128)} custom-call(f32[2048,1024]{1,0:T(8,128)} %rx.1, f32[2048,1024]{1,0:T(8,128)} %rg.1, f32[128,1024]{1,0:T(8,128)} %qx.1, f32[128,1024]{1,0:T(8,128)} %qg.1), custom_call_target="tpu_custom_call" | custom-call | tf_op jit(solution)/shard_map/pallas_call | solution.py:300
  91.3 1.9 %copy.6 = f32[128,1024]{1,0:T(8,128)} copy(f32[128,1024]{1,0:T(8,128)} %shard_map.46) | data formatting | bytes 1048576

commit v5 on v4

--- a/solution.py
+++ b/solution.py
@@ -17,11 +17,11 @@
 LAST = "ZCWYWZZYZYZYZZZZZ"
 UNITS = 16
 REL = (2, 1, 3, 0)
-STAGES = 16
+STAGES = 14
 PARTS = ((0, 1), (1, 3), (3, 4))
 
 
-def kernel(rx, rg, qx, qg, out, rh, rl, qbuf, qcat, stage, pbuf, csum, y1, y2, zin, zfirst,
+def kernel(rx, rg, qx, qg, out_x, out_g, rh, rl, qbuf, qcat, stage, pbuf, csum, y1, y2, zin, zfirst,
            load_sem, stage_sem, ag_send, ag_recv, c_send, c_recv, y1_send, y1_recv, y2_send, y2_recv, z_send, z_recv, first_send, first_recv):
     t, w = lax.axis_index("tok"), lax.axis_index("wid")
     zh, x = t // 4, t % 4
@@ -57,7 +57,7 @@
 
     def load(matrix, s, half):
         row = pl.multiple_of(half * 1024 + ((y + REL[s]) % 4) * 256, 256)
-        slot = matrix * 8 + s * 2 + half
+        slot = (matrix * 8 + s * 2 + half) % STAGES
         return pltpu.make_async_copy((rx, rg)[matrix].at[pl.ds(row, 256)], stage.at[slot], stage_sem.at[slot])
 
     def split(matrix, *parts):
@@ -66,7 +66,7 @@
                 load(matrix, s, half).wait()
         for s in parts:
             for half in range(2):
-                value = stage[matrix * 8 + s * 2 + half]
+                value = stage[(matrix * 8 + s * 2 + half) % STAGES]
                 hi = value.astype(BF16)
                 rh[matrix, s, pl.ds(half * 256, 256)] = hi
                 rl[matrix, s, pl.ds(half * 256, 256)] = (value - hi.astype(F32)).astype(BF16)
@@ -77,7 +77,7 @@
         pl.semaphore_signal(barrier, inc=1, device_id=other, device_id_type=MESH)
     mine = [pltpu.make_async_copy(qx, qbuf.at[0], load_sem.at[0]), pltpu.make_async_copy(qg, qbuf.at[1], load_sem.at[1])]
     mine[0].start()
-    for matrix, s in ((0, 0), (0, 1), (0, 2), (1, 0), (0, 3), (1, 1), (1, 2), (1, 3)):
+    for matrix, s in ((0, 0), (0, 1), (0, 2), (1, 0), (0, 3), (1, 1), (1, 2)):
         for half in range(2):
             load(matrix, s, half).start()
         if (matrix, s) == (0, 0):
@@ -175,6 +175,8 @@
     mine[0].wait()
     queries(0, 0)
     split(0, 0)
+    for half in range(2):
+        load(1, 3, half).start()
     dots(0, 0, 0, 1)
     pl.semaphore_wait(barrier, len(others))
     send(0, 0, 1)
@@ -273,19 +275,17 @@
         z_copy(u).wait_recv()
         return csum[u, 3, zl] + zin[u]
 
-    def store(dx, flip, value):
+    def store(out, dx, flip, value):
         source = ((zh + flip) % 2) * 4 + (x + dx) % 4
         out[:, pl.ds(pl.multiple_of(source * 128, 128), 128)] = value
 
-    def finish(block):
-        first, second, dx, flip = block
-        store(dx, flip, gram(first) * gram(second))
-
-    halves = gram(2) * gram(5), gram(3) * gram(6)
-    store(3, 0, jnp.concatenate([half[:, :64] for half in halves], axis=1))
-    store(1, 0, jnp.concatenate([half[:, 64:] for half in halves], axis=1))
-    for block in sorted(BLOCKS, key=lambda block: max(done.index(u) for u in block[:2])):
-        finish(block)
+    for out, first, second in ((out_x, 2, 3), (out_g, 5, 6)):
+        halves = gram(first), gram(second)
+        store(out, 3, 0, jnp.concatenate([half[:, :64] for half in halves], axis=1))
+        store(out, 1, 0, jnp.concatenate([half[:, 64:] for half in halves], axis=1))
+    places = {u: (out, dx, flip) for *units, dx, flip in BLOCKS for u, out in zip(units, (out_x, out_g))}
+    for u in sorted(places, key=done.index):
+        store(*places[u], gram(u))
 
     for u in (last - 1, last):
         core_copy(u, 0, 4).wait_send()
@@ -297,11 +297,11 @@
 
 def per_device(resident_x, resident_g, query_x, query_g):
     dma = pltpu.SemaphoreType.DMA
-    return pl.pallas_call(
+    input_gram, grad_gram = pl.pallas_call(
         kernel,
-        out_shape=jax.ShapeDtypeStruct((128, 1024), F32),
+        out_shape=[jax.ShapeDtypeStruct((128, 1024), F32)] * 2,
         in_specs=[pl.BlockSpec(memory_space=pl.ANY)] * 4,
-        out_specs=pl.BlockSpec(memory_space=pltpu.VMEM),
+        out_specs=[pl.BlockSpec(memory_space=pltpu.VMEM)] * 2,
         scratch_shapes=[
             pltpu.VMEM((2, 4, 512, 1024), BF16),
             pltpu.VMEM((2, 4, 512, 1024), BF16),
@@ -319,6 +319,7 @@
         ],
         compiler_params=pltpu.CompilerParams(collective_id=0, has_side_effects=True, vmem_limit_bytes=61 * 2**20),
     )(resident_x, resident_g, query_x, query_g)
+    return input_gram * grad_gram
 
 
 def solution(mesh):

time: 93.4 us -> 93 us (level)
  other arithmetic: 0 us -> 2.06 us
  local copies, waits for them, and re-layouts: 1.89 us -> 0 us
    mul x0 -> x1, other arithmetic: none -> 2.06 us  [per_device(): return input_gram * grad_gram]
    unnamed x1 -> x0, local copies, waits for them, and re-layouts: 1.89 us -> none
where the time goes in v5:
time: 93 us; the launch traced here: 92.9 us
  Pallas kernels  90.8 us (98%)
  other arithmetic  2.06 us (2%)
    pallas_call x1, Pallas kernels, per_device(): pl.pallas_call(kernel, out_shape=[jax.ShapeDtypeStruct((128, 1024), F32)]...  90.8 us
    mul x1, other arithmetic, per_device(): return input_gram * grad_gram  2.06 us

profile of v5, /device:TPU:0, one launch (start us, length us, event | category | flops | bytes accessed | tf_op | source)
XLA Modules:
  0.0 92.9 jit_solution(7133971147151592871)
XLA Ops:
  0.0 90.8 %shard_map.46 = (f32[128,1024]{1,0:T(8,128)}, f32[128,1024]{1,0:T(8,128)}) custom-call(f32[2048,1024]{1,0:T(8,128)} %rx.1, f32[2048,1024]{1,0:T(8,128)} %rg.1, f32[128,1024]{1,0:T(8,128)} %qx.1, f32[128,1024]{1,0:T(8,128)} %qg.1), custom_call_target="tpu_custom_call" | custom-call | tf_op jit(solution)/shard_map/pallas_call | solution.py:300
  90.8 2.1 %mul.3 = f32[128,1024]{1,0:T(8,128)} multiply(f32[128,1024]{1,0:T(8,128)} %get-tuple-element.7, f32[128,1024]{1,0:T(8,128)} %get-tuple-element.8) | non-fusion elementwise | flops 131072 | bytes 1572864 | tf_op jit(solution)/shard_map/mul | solution.py:322

commit v6 on v5

--- a/solution.py
+++ b/solution.py
@@ -13,8 +13,8 @@
 
 BLOCKS = ((0, 1, 0, 0), (4, 7, 0, 1), (8, 11, 2, 0), (9, 12, 3, 1), (10, 13, 1, 1), (14, 15, 2, 1))
 ACROSS_FIRST = (11, 13)
-STEPS = ("CyAY", "ACyZW", "yACy", "ACZW", "yACyZ", "ACyW", "ACYCZZZ", "YCAYW", "YAYW", "CyAyC", "AyC", "ACY", "ACYZ", "yAyC")
-LAST = "ZCWYWZZYZYZYZZZZZ"
+STEPS = ("Ay", "Ay", "yCACYZ", "AC", "A", "YCACYCZ", "CyACYZZZW", "CyAy", "ACW", "YAyCZ", "AyC", "Ay", "CYACY", "ACy")
+LAST = "CWZZYZZWZYZZYYZZZZZZ"
 UNITS = 16
 REL = (2, 1, 3, 0)
 STAGES = 14

time: 93 us -> 92.2 us (level)
  no operation moved by 1% of the time
where the time goes in v6:
time: 92.2 us; the launch traced here: 92.1 us
  Pallas kernels  90 us (98%)
  other arithmetic  2.06 us (2%)
    pallas_call x1, Pallas kernels, per_device(): pl.pallas_call(kernel, out_shape=[jax.ShapeDtypeStruct((128, 1024), F32)]...  90 us
    mul x1, other arithmetic, per_device(): return input_gram * grad_gram  2.06 us

profile of v6, /device:TPU:0, one launch (start us, length us, event | category | flops | bytes accessed | tf_op | source)
XLA Modules:
  0.0 92.1 jit_solution(10729056172645135411)
XLA Ops:
  0.0 90.0 %shard_map.46 = (f32[128,1024]{1,0:T(8,128)}, f32[128,1024]{1,0:T(8,128)}) custom-call(f32[2048,1024]{1,0:T(8,128)} %rx.1, f32[2048,1024]{1,0:T(8,128)} %rg.1, f32[128,1024]{1,0:T(8,128)} %qx.1, f32[128,1024]{1,0:T(8,128)} %qg.1), custom_call_target="tpu_custom_call" | custom-call | tf_op jit(solution)/shard_map/pallas_call | solution.py:300
  90.0 2.1 %mul.3 = f32[128,1024]{1,0:T(8,128)} multiply(f32[128,1024]{1,0:T(8,128)} %get-tuple-element.7, f32[128,1024]{1,0:T(8,128)} %get-tuple-element.8) | non-fusion elementwise | flops 131072 | bytes 1572864 | tf_op jit(solution)/shard_map/mul | solution.py:322
